TPU v7x, 32 devices: a whole 2x2x4 slice. The times are simulated.
32 devices in a mesh: lat: 4 (over z), lon: 8 (over y, x, core).
Axes of the slice: x: 2, y: 2, z: 4, core: 2. Of those that a mesh axis runs over, the one named last changes fastest.
Arguments:
- covariance: float32 [4, 4, 128, 128], P('lat', None, 'lon'), may hold values from -6 to 6
- winds: float32 [2, 3, 4, 128], P(None, None, None, 'lon'), may hold values from -0.35 to 0.35
- diffusivity: float32 [4, 128], P(None, 'lon'), may hold values from 0.01 to 0.07
- cutoff: int32 [4], replicated, may hold values from 0 to 1, as said below
Outputs:
- forecast: float32 [4, 4, 128, 128], P('lat', None, 'lon')
Inputs may be any that keep to these rules, and one draw needn't show every extreme that they name: Some latitude has cutoff 1 and some other has 0.
All inputs are finite; a program needn't handle non-finite values.
Results may differ from a plain program's by a relative error of at most 0.00002.
Values sent between devices are 32-bit elements; how exact they have to be, the bound alone decides.
No kernel may reach another device: no remote copies, remote signals or barrier semaphores. Data moves between devices by JAX's collectives and lax.ppermute only.
A program may use at most 192 MiB of HBM per device.

v0:
```python
import jax
import jax.numpy as jnp
from jax import lax
from jax.sharding import PartitionSpec as P

STEPS = 3


def extended_2(block, sides, width):
    for axis, dim in sides:
        count = lax.axis_size(axis)
        forward = [(i, i + 1) for i in range(count - 1)]
        forward.append((count - 1, 0))
        backward = [(target, source) for source, target in forward]
        low = lax.ppermute(
            lax.slice_in_dim(block, block.shape[dim] - width, None, axis=dim), axis, forward
        )
        high = lax.ppermute(lax.slice_in_dim(block, 0, width, axis=dim), axis, backward)
        block = jnp.concatenate([low, block, high], axis=dim)
    return block


def from_behind(shard, axis, by):
    length = lax.axis_size(axis)
    pairs = [(i, i + by) for i in range(length) if 0 <= i + by < length]
    return lax.ppermute(shard, axis, pairs)


def advance(extended, east_wind, north_wind, spread):
    center = extended[:, :, 1:-1]
    western = extended[:, :, :-2]
    eastern = extended[:, :, 2:]
    zeros_row = jnp.zeros_like(center[:, :1])
    southern = jnp.concatenate([zeros_row, center[:, :-1]], axis=1)
    northern = jnp.concatenate([center[:, 1:], zeros_row], axis=1)
    east_wind = east_wind[None, :, :, None]
    north_wind = north_wind[None, :, :, None]
    spread = spread[None, :, :, None]
    transport = (
        jnp.maximum(east_wind, 0.0) * (center - western)
        + jnp.minimum(east_wind, 0.0) * (eastern - center)
        + jnp.maximum(north_wind, 0.0) * (center - southern)
        + jnp.minimum(north_wind, 0.0) * (northern - center)
    )
    return center - transport + spread * (eastern + western + northern + southern - 4.0 * center)


def propagate(state_field, widened):
    lon_local = state_field.shape[2]
    extended = extended_2(state_field, (("lon", 2),), STEPS)
    for substep in range(STEPS):
        out_width = lon_local + 2 * (STEPS - substep - 1)
        offset_at = substep + 1
        extended = advance(
            extended,
            widened[substep, :, offset_at : offset_at + out_width],
            widened[STEPS + substep, :, offset_at : offset_at + out_width],
            widened[2 * STEPS, :, offset_at : offset_at + out_width],
        )
    return extended


def relayout(block, reach_rows):
    row_count = block.shape[0]
    lat_count = block.shape[1]
    swapped = lax.all_to_all(block, "lon", split_axis=3, concat_axis=2, tiled=True)
    lon_count = swapped.shape[2]
    col_count = swapped.shape[3]
    block_count = lat_count // row_count
    device_index = lax.axis_index("lat")
    reach_blocks = min((reach_rows + row_count - 1) // row_count, block_count - 1)
    tile_blocks = swapped.reshape(row_count, block_count, row_count, lon_count, col_count)

    def piece_for(offset):
        target = jnp.clip(device_index + offset, 0, block_count - 1)
        return lax.dynamic_index_in_dim(tile_blocks, target, axis=1, keepdims=False)

    own_piece = piece_for(0)
    received = []
    for offset in range(-reach_blocks, reach_blocks + 1):
        if offset == 0:
            received.append(own_piece)
        else:
            received.append(from_behind(piece_for(offset), "lat", offset))
    window = jnp.stack(received[::-1], axis=0)
    padded = jnp.zeros(
        (block_count + 2 * reach_blocks, row_count, row_count, lon_count, col_count), jnp.float32
    )
    padded = lax.dynamic_update_slice_in_dim(padded, window, device_index, 0)
    regrouped = padded[reach_blocks : reach_blocks + block_count].reshape(
        lat_count, row_count, lon_count, col_count
    )
    return jnp.transpose(regrouped, (1, 0, 3, 2))


def per_device(covariance, winds, diffusivity, cutoff):
    row_count = covariance.shape[0]
    lat_count = covariance.shape[1]
    lon_local = covariance.shape[2]
    band_rows = lat_count // 4
    device_index = lax.axis_index("lat")
    lat_local = device_index * row_count + jnp.arange(row_count, dtype=jnp.int32)
    lat_all = jnp.arange(lat_count, dtype=jnp.int32)
    cut_local = lax.dynamic_slice_in_dim(cutoff, device_index * row_count, row_count)
    keep_first = jnp.abs(lat_all[None, :] - lat_local[:, None]) <= cutoff[None, :]
    keep_second = jnp.abs(lat_all[None, :] - lat_local[:, None]) <= cut_local[:, None]
    stacked = jnp.concatenate(
        [winds.reshape(2 * STEPS, lat_count, lon_local), diffusivity[None]], axis=0
    )
    widened = extended_2(stacked, (("lon", 2),), STEPS)
    state_field = jnp.where(keep_first[:, :, None, None], covariance, 0.0)
    state_field = propagate(state_field, widened)
    state_field = relayout(state_field, band_rows + STEPS)
    state_field = propagate(state_field, widened)
    state_field = jnp.where(keep_second[:, :, None, None], state_field, 0.0)
    return relayout(state_field, band_rows)


def solution(mesh):
    in_specs = (P("lat", None, "lon", None), P(None, None, None, "lon"), P(None, "lon"), P())
    out_specs = P("lat", None, "lon", None)
    return jax.shard_map(
        per_device, mesh=mesh, in_specs=in_specs, out_specs=out_specs, check_vma=False
    )
```

profile of v0, /device:TPU:0, one launch (start us, length us, event | category | flops | bytes accessed | tf_op | source)
XLA Modules:
  0.0 67.6 jit_solution(5714886319299607555)
XLA Ops:
  0.0 0.7 copy-done.2
  0.7 0.6 dynamic_slice.34
  1.2 0.7 fusion.50
  1.9 0.8 %broadcast_select_fusion = f32[1,4,16,128]{3,2,1,0:T(8,128)S(1)} fusion(f32[1,4,16,128]{3,2,1,0:T(8,128)} %param.4, pred[4]{0:T(512)(128)(4,1)S(1)} %get-tuple-element.51), kind=kLoop, calls=%fused_computation.86 | loop fusion | flops 8192 | bytes 65540 | tf_op jit(solution)/shard_map/jit(_where)/select_n | solution.py:111
  2.7 0.5 collective-permute-start
  3.3 2.9 %collective-permute-start.1 = (f32[1,4,3,128]{3,2,1,0:T(4,128)S(1)}, f32[1,4,3,128]{3,2,1,0:T(4,128)S(1)}, u32[]{:S(2)}, u32[]{:S(2)}) collective-permute-start(f32[1,4,3,128]{3,2,1,0:T(4,128)S(1)} %get-tuple-element.44), channel_id=1, source_target_pairs={{1,0},{2,1},{3,2},{4,3},{5,4},{6,5},{7,6},{0,7},{9,8},{10,9},{11,1... | collective-permute-start | bytes 18440 | tf_op jit(solution)/shard_map/ppermute | solution.py:18
  6.3 0.3 collective-permute-start.2
  6.6 2.3 %collective-permute-start.3 = (f32[7,4,3]{2,1,0:T(4,128)S(1)}, f32[7,4,3]{2,1,0:T(4,128)S(1)}, u32[]{:S(2)}, u32[]{:S(2)}) collective-permute-start(f32[7,4,3]{2,1,0:T(4,128)S(1)} %get-tuple-element.46), channel_id=1, source_target_pairs={{1,0},{2,1},{3,2},{4,3},{5,4},{6,5},{7,6},{0,7},{9,8},{10,9},{11,1... | collective-permute-start | bytes 1016 | tf_op jit(solution)/shard_map/ppermute | solution.py:18
  9.0 1.4 %collective-permute-done.2 = f32[7,4,3]{2,1,0:T(4,128)S(1)} collective-permute-done((f32[7,4,3]{2,1,0:T(4,128)S(1)}, f32[7,4,3]{2,1,0:T(4,128)S(1)}, u32[]{:S(2)}, u32[]{:S(2)}) %collective-permute-start.2) | collective-permute-done | bytes 368 | tf_op jit(solution)/shard_map/ppermute | solution.py:15
  10.5 0.1 maximum_bitcast_fusion.4
  10.6 0.1 fusion.4
  10.8 0.1 fusion.12
  10.9 0.1 fusion.36
  11.0 0.1 copy.36
  11.2 0.8 %reshape.186 = f32[8,1,1024]{2,1,0:T(1,128)} reshape(f32[128,1,4,16]{3,2,1,0:T(4,128)S(1)} %bitcast.89) | data formatting | bytes 65536
  12.0 4.6 %all-to-all-start = ((f32[8,1,1024]{2,1,0:T(1,128)}), f32[8,1,1024]{2,1,0:T(1,128)S(1)}, u32[]{:S(2)}, u32[]{:S(2)}) async-start(f32[8,1,1024]{2,1,0:T(1,128)} %reshape.186), calls=%async_computation | async-start | bytes 65536 | tf_op jit(solution)/shard_map/all_to_all | solution.py:66
  16.7 4.8 %all-to-all-done = f32[8,1,1024]{2,1,0:T(1,128)S(1)} async-done(((f32[8,1,1024]{2,1,0:T(1,128)}), f32[8,1,1024]{2,1,0:T(1,128)S(1)}, u32[]{:S(2)}, u32[]{:S(2)}) %all-to-all-start) | async-done | bytes 32800 | tf_op jit(solution)/shard_map/all_to_all | solution.py:66
  21.5 0.5 broadcast.178
  22.0 0.7 %reduce = f32[8,1024]{1,0:T(8,128)S(1)} reduce(f32[8,1,1024]{2,1,0:T(1,128)S(1)} %all-to-all-done, f32[]{:T(128)} %broadcast.178), dimensions={1}, to_apply=%all_to_all.22.reduce_sub_computation | reduce | bytes 65540 | tf_op jit(solution)/shard_map/all_to_all | solution.py:66
  22.7 0.2 reshape.187
  23.0 0.2 copy.37
  23.1 0.1 reshape.182
  23.3 5.5 %collective-permute-start.4 = (f32[1,1,128,16]{2,3,1,0:T(8,128)S(1)}, f32[1,1,128,16]{2,3,1,0:T(8,128)S(1)}, u32[]{:S(2)}, u32[]{:S(2)}) collective-permute-start(f32[1,1,128,16]{2,3,1,0:T(8,128)S(1)} %get-tuple-element.42), channel_id=1, source_target_pairs={{0,24},{1,25},{2,26},{3,27},{4,28},{5,29},{6,30},{7,31}} | collective-permute-start | bytes 24584 | tf_op jit(solution)/shard_map/ppermute | solution.py:26
  28.8 1.3 %collective-permute-start.5 = (f32[1,1,128,16]{2,3,1,0:T(8,128)S(1)}, f32[1,1,128,16]{2,3,1,0:T(8,128)S(1)}, u32[]{:S(2)}, u32[]{:S(2)}) collective-permute-start(f32[1,1,128,16]{2,3,1,0:T(8,128)S(1)} %get-tuple-element.41), channel_id=1, source_target_pairs={{0,16},{8,24},{1,17},{9,25},{2,18},{10,26},{3,19},{11,27},{4,20},{... | collective-permute-start | bytes 24584 | tf_op jit(solution)/shard_map/ppermute | solution.py:26
  30.1 2.5 %collective-permute-start.6 = (f32[1,1,128,16]{2,3,1,0:T(8,128)S(1)}, f32[1,1,128,16]{2,3,1,0:T(8,128)S(1)}, u32[]{:S(2)}, u32[]{:S(2)}) collective-permute-start(f32[1,1,128,16]{2,3,1,0:T(8,128)S(1)} %get-tuple-element.40), channel_id=1, source_target_pairs={{0,8},{8,16},{16,24},{1,9},{9,17},{17,25},{2,10},{10,18},{18,26},{... | collective-permute-start | bytes 24584 | tf_op jit(solution)/shard_map/ppermute | solution.py:26
  32.6 1.3 %collective-permute-done.6 = f32[1,1,128,16]{2,3,1,0:T(8,128)S(1)} collective-permute-done((f32[1,1,128,16]{2,3,1,0:T(8,128)S(1)}, f32[1,1,128,16]{2,3,1,0:T(8,128)S(1)}, u32[]{:S(2)}, u32[]{:S(2)}) %collective-permute-start.6) | collective-permute-done | bytes 8224 | tf_op jit(solution)/shard_map/ppermute | solution.py:26
  33.9 1.3 %collective-permute-start.7 = (f32[1,1,128,16]{2,3,1,0:T(8,128)S(1)}, f32[1,1,128,16]{2,3,1,0:T(8,128)S(1)}, u32[]{:S(2)}, u32[]{:S(2)}) collective-permute-start(f32[1,1,128,16]{2,3,1,0:T(8,128)S(1)} %get-tuple-element.38), channel_id=1, source_target_pairs={{8,0},{16,8},{24,16},{9,1},{17,9},{25,17},{10,2},{18,10},{26,18},{... | collective-permute-start | bytes 24584 | tf_op jit(solution)/shard_map/ppermute | solution.py:26
  35.2 1.3 %collective-permute-start.8 = (f32[1,1,128,16]{2,3,1,0:T(8,128)S(1)}, f32[1,1,128,16]{2,3,1,0:T(8,128)S(1)}, u32[]{:S(2)}, u32[]{:S(2)}) collective-permute-start(f32[1,1,128,16]{2,3,1,0:T(8,128)S(1)} %get-tuple-element.37), channel_id=1, source_target_pairs={{16,0},{24,8},{17,1},{25,9},{18,2},{26,10},{19,3},{27,11},{20,4},{... | collective-permute-start | bytes 24584 | tf_op jit(solution)/shard_map/ppermute | solution.py:26
  36.5 1.3 %collective-permute-start.9 = (f32[1,1,128,16]{2,3,1,0:T(8,128)S(1)}, f32[1,1,128,16]{2,3,1,0:T(8,128)S(1)}, u32[]{:S(2)}, u32[]{:S(2)}) collective-permute-start(f32[1,1,128,16]{2,3,1,0:T(8,128)S(1)} %get-tuple-element.36), channel_id=1, source_target_pairs={{24,0},{25,1},{26,2},{27,3},{28,4},{29,5},{30,6},{31,7}} | collective-permute-start | bytes 24584 | tf_op jit(solution)/shard_map/ppermute | solution.py:26
  37.8 1.9 %collective-permute-done.7 = f32[1,1,128,16]{2,3,1,0:T(8,128)S(1)} collective-permute-done((f32[1,1,128,16]{2,3,1,0:T(8,128)S(1)}, f32[1,1,128,16]{2,3,1,0:T(8,128)S(1)}, u32[]{:S(2)}, u32[]{:S(2)}) %collective-permute-start.7) | collective-permute-done | bytes 8224 | tf_op jit(solution)/shard_map/ppermute | solution.py:26
  39.7 2.7 %collective-permute-done.8 = f32[1,1,128,16]{2,3,1,0:T(8,128)S(1)} collective-permute-done((f32[1,1,128,16]{2,3,1,0:T(8,128)S(1)}, f32[1,1,128,16]{2,3,1,0:T(8,128)S(1)}, u32[]{:S(2)}, u32[]{:S(2)}) %collective-permute-start.8) | collective-permute-done | bytes 8224 | tf_op jit(solution)/shard_map/ppermute | solution.py:26
  42.5 2.8 %collective-permute-done.9 = f32[1,1,128,16]{2,3,1,0:T(8,128)S(1)} collective-permute-done((f32[1,1,128,16]{2,3,1,0:T(8,128)S(1)}, f32[1,1,128,16]{2,3,1,0:T(8,128)S(1)}, u32[]{:S(2)}, u32[]{:S(2)}) %collective-permute-start.9) | collective-permute-done | bytes 8224 | tf_op jit(solution)/shard_map/ppermute | solution.py:26
  45.4 2.6 %collective-permute-start.11 = (f32[1,4,3,128]{3,2,1,0:T(4,128)S(1)}, f32[1,4,3,128]{3,2,1,0:T(4,128)S(1)}, u32[]{:S(2)}, u32[]{:S(2)}) collective-permute-start(f32[1,4,3,128]{3,2,1,0:T(4,128)S(1)} %get-tuple-element.35), channel_id=1, source_target_pairs={{1,0},{2,1},{3,2},{4,3},{5,4},{6,5},{7,6},{0,7},{9,8},{10,9},{11,1... | collective-permute-start | bytes 18440 | tf_op jit(solution)/shard_map/ppermute | solution.py:18
  48.1 1.4 %collective-permute-done.10 = f32[1,4,3,128]{3,2,1,0:T(4,128)S(1)} collective-permute-done((f32[1,4,3,128]{3,2,1,0:T(4,128)S(1)}, f32[1,4,3,128]{3,2,1,0:T(4,128)S(1)}, u32[]{:S(2)}, u32[]{:S(2)}) %collective-permute-start.10) | collective-permute-done | bytes 6176 | tf_op jit(solution)/shard_map/ppermute | solution.py:15
  49.5 0.1 fusion.20
  49.6 0.1 fusion.28
  49.8 0.1 fusion.45
  49.9 0.1 copy.39
  50.1 0.2 reshape.188
  50.3 8.5 %all_to_all.30 = f32[8,1,1024]{2,1,0:T(1,128)S(1)} all-to-all(f32[8,1,1024]{2,1,0:T(1,128)S(1)} %reshape.188), channel_id=1, replica_groups=mesh['lat'=4,'lon'=8] {'lon'}, dimensions={0} | all-to-all | bytes 65536 | tf_op jit(solution)/shard_map/all_to_all | solution.py:66
  58.8 0.7 %reduce.1 = f32[8,1024]{1,0:T(8,128)S(1)} reduce(f32[8,1,1024]{2,1,0:T(1,128)S(1)} %all_to_all.30, f32[]{:T(128)} %broadcast.178), dimensions={1}, to_apply=%all_to_all.25.reduce_sub_computation | reduce | bytes 65540 | tf_op jit(solution)/shard_map/all_to_all | solution.py:66
  59.5 0.2 reshape.189
  59.8 0.2 copy.40
  59.9 0.1 reshape.184
  60.1 1.3 %collective-permute-start.12 = (f32[1,1,128,16]{2,3,1,0:T(8,128)S(1)}, f32[1,1,128,16]{2,3,1,0:T(8,128)S(1)}, u32[]{:S(2)}, u32[]{:S(2)}) collective-permute-start(f32[1,1,128,16]{2,3,1,0:T(8,128)S(1)} %get-tuple-element.31), channel_id=1, source_target_pairs={{0,8},{8,16},{16,24},{1,9},{9,17},{17,25},{2,10},{10,18},{18,26},{... | collective-permute-start | bytes 24584 | tf_op jit(solution)/shard_map/ppermute | solution.py:26
  61.4 1.3 %collective-permute-start.13 = (f32[1,1,128,16]{2,3,1,0:T(8,128)S(1)}, f32[1,1,128,16]{2,3,1,0:T(8,128)S(1)}, u32[]{:S(2)}, u32[]{:S(2)}) collective-permute-start(f32[1,1,128,16]{2,3,1,0:T(8,128)S(1)} %get-tuple-element.32), channel_id=1, source_target_pairs={{8,0},{16,8},{24,16},{9,1},{17,9},{25,17},{10,2},{18,10},{26,18},{... | collective-permute-start | bytes 24584 | tf_op jit(solution)/shard_map/ppermute | solution.py:26
  62.7 4.2 %collective-permute-done.13 = f32[1,1,128,16]{2,3,1,0:T(8,128)S(1)} collective-permute-done((f32[1,1,128,16]{2,3,1,0:T(8,128)S(1)}, f32[1,1,128,16]{2,3,1,0:T(8,128)S(1)}, u32[]{:S(2)}, u32[]{:S(2)}) %collective-permute-start.13) | collective-permute-done | bytes 8224 | tf_op jit(solution)/shard_map/ppermute | solution.py:26
  66.9 0.6 slice_bitcast_fusion
  (42 shorter events, 0.5 us)
Async XLA Ops:
  0.0 0.7 copy-start.2
  2.7 3.5 %copy-start = (f32[2,3,4,16]{3,2,1,0:T(4,128)S(1)}, f32[2,3,4,16]{3,2,1,0:T(4,128)}, u32[]{:S(2)}) copy-start(f32[2,3,4,16]{3,2,1,0:T(4,128)} %param.5) | copy-start | bytes 4612
  2.7 7.8 %collective-permute-start = (f32[1,4,3,128]{3,2,1,0:T(4,128)S(1)}, f32[1,4,3,128]{3,2,1,0:T(4,128)S(1)}, u32[]{:S(2)}, u32[]{:S(2)}) collective-permute-start(f32[1,4,3,128]{3,2,1,0:T(4,128)S(1)} %get-tuple-element.43), channel_id=1, source_target_pairs={{0,1},{1,2},{2,3},{3,4},{4,5},{5,6},{6,7},{7,0},{8,9},{9,10},{10,1... | collective-permute-start | bytes 18440 | tf_op jit(solution)/shard_map/ppermute | solution.py:15
  3.3 3.0 %copy-start.1 = (f32[4,16]{1,0:T(4,128)S(1)}, f32[4,16]{1,0:T(4,128)}, u32[]{:S(2)}) copy-start(f32[4,16]{1,0:T(4,128)} %param.6) | copy-start | bytes 772
  3.3 7.3 %collective-permute-start.1 = (f32[1,4,3,128]{3,2,1,0:T(4,128)S(1)}, f32[1,4,3,128]{3,2,1,0:T(4,128)S(1)}, u32[]{:S(2)}, u32[]{:S(2)}) collective-permute-start(f32[1,4,3,128]{3,2,1,0:T(4,128)S(1)} %get-tuple-element.44), channel_id=1, source_target_pairs={{1,0},{2,1},{3,2},{4,3},{5,4},{6,5},{7,6},{0,7},{9,8},{10,9},{11,1... | collective-permute-start | bytes 18440 | tf_op jit(solution)/shard_map/ppermute | solution.py:18
  6.3 4.0 %collective-permute-start.2 = (f32[7,4,3]{2,1,0:T(4,128)S(1)}, f32[7,4,3]{2,1,0:T(4,128)S(1)}, u32[]{:S(2)}, u32[]{:S(2)}) collective-permute-start(f32[7,4,3]{2,1,0:T(4,128)S(1)} %get-tuple-element.45), channel_id=1, source_target_pairs={{0,1},{1,2},{2,3},{3,4},{4,5},{5,6},{6,7},{7,0},{8,9},{9,10},{10,1... | collective-permute-start | bytes 1016 | tf_op jit(solution)/shard_map/ppermute | solution.py:15
  6.6 3.8 %collective-permute-start.3 = (f32[7,4,3]{2,1,0:T(4,128)S(1)}, f32[7,4,3]{2,1,0:T(4,128)S(1)}, u32[]{:S(2)}, u32[]{:S(2)}) collective-permute-start(f32[7,4,3]{2,1,0:T(4,128)S(1)} %get-tuple-element.46), channel_id=1, source_target_pairs={{1,0},{2,1},{3,2},{4,3},{5,4},{6,5},{7,6},{0,7},{9,8},{10,9},{11,1... | collective-permute-start | bytes 1016 | tf_op jit(solution)/shard_map/ppermute | solution.py:18
  12.0 9.5 %all-to-all-start = ((f32[8,1,1024]{2,1,0:T(1,128)}), f32[8,1,1024]{2,1,0:T(1,128)S(1)}, u32[]{:S(2)}, u32[]{:S(2)}) async-start(f32[8,1,1024]{2,1,0:T(1,128)} %reshape.186), calls=%async_computation | async-start | bytes 65536 | tf_op jit(solution)/shard_map/all_to_all | solution.py:66
  23.3 9.3 %collective-permute-start.4 = (f32[1,1,128,16]{2,3,1,0:T(8,128)S(1)}, f32[1,1,128,16]{2,3,1,0:T(8,128)S(1)}, u32[]{:S(2)}, u32[]{:S(2)}) collective-permute-start(f32[1,1,128,16]{2,3,1,0:T(8,128)S(1)} %get-tuple-element.42), channel_id=1, source_target_pairs={{0,24},{1,25},{2,26},{3,27},{4,28},{5,29},{6,30},{7,31}} | collective-permute-start | bytes 24584 | tf_op jit(solution)/shard_map/ppermute | solution.py:26
  28.8 3.8 %collective-permute-start.5 = (f32[1,1,128,16]{2,3,1,0:T(8,128)S(1)}, f32[1,1,128,16]{2,3,1,0:T(8,128)S(1)}, u32[]{:S(2)}, u32[]{:S(2)}) collective-permute-start(f32[1,1,128,16]{2,3,1,0:T(8,128)S(1)} %get-tuple-element.41), channel_id=1, source_target_pairs={{0,16},{8,24},{1,17},{9,25},{2,18},{10,26},{3,19},{11,27},{4,20},{... | collective-permute-start | bytes 24584 | tf_op jit(solution)/shard_map/ppermute | solution.py:26
  30.1 3.8 %collective-permute-start.6 = (f32[1,1,128,16]{2,3,1,0:T(8,128)S(1)}, f32[1,1,128,16]{2,3,1,0:T(8,128)S(1)}, u32[]{:S(2)}, u32[]{:S(2)}) collective-permute-start(f32[1,1,128,16]{2,3,1,0:T(8,128)S(1)} %get-tuple-element.40), channel_id=1, source_target_pairs={{0,8},{8,16},{16,24},{1,9},{9,17},{17,25},{2,10},{10,18},{18,26},{... | collective-permute-start | bytes 24584 | tf_op jit(solution)/shard_map/ppermute | solution.py:26
  33.9 5.8 %collective-permute-start.7 = (f32[1,1,128,16]{2,3,1,0:T(8,128)S(1)}, f32[1,1,128,16]{2,3,1,0:T(8,128)S(1)}, u32[]{:S(2)}, u32[]{:S(2)}) collective-permute-start(f32[1,1,128,16]{2,3,1,0:T(8,128)S(1)} %get-tuple-element.38), channel_id=1, source_target_pairs={{8,0},{16,8},{24,16},{9,1},{17,9},{25,17},{10,2},{18,10},{26,18},{... | collective-permute-start | bytes 24584 | tf_op jit(solution)/shard_map/ppermute | solution.py:26
  35.2 7.3 %collective-permute-start.8 = (f32[1,1,128,16]{2,3,1,0:T(8,128)S(1)}, f32[1,1,128,16]{2,3,1,0:T(8,128)S(1)}, u32[]{:S(2)}, u32[]{:S(2)}) collective-permute-start(f32[1,1,128,16]{2,3,1,0:T(8,128)S(1)} %get-tuple-element.37), channel_id=1, source_target_pairs={{16,0},{24,8},{17,1},{25,9},{18,2},{26,10},{19,3},{27,11},{20,4},{... | collective-permute-start | bytes 24584 | tf_op jit(solution)/shard_map/ppermute | solution.py:26
  36.5 8.8 %collective-permute-start.9 = (f32[1,1,128,16]{2,3,1,0:T(8,128)S(1)}, f32[1,1,128,16]{2,3,1,0:T(8,128)S(1)}, u32[]{:S(2)}, u32[]{:S(2)}) collective-permute-start(f32[1,1,128,16]{2,3,1,0:T(8,128)S(1)} %get-tuple-element.36), channel_id=1, source_target_pairs={{24,0},{25,1},{26,2},{27,3},{28,4},{29,5},{30,6},{31,7}} | collective-permute-start | bytes 24584 | tf_op jit(solution)/shard_map/ppermute | solution.py:26
  45.4 4.1 %collective-permute-start.10 = (f32[1,4,3,128]{3,2,1,0:T(4,128)S(1)}, f32[1,4,3,128]{3,2,1,0:T(4,128)S(1)}, u32[]{:S(2)}, u32[]{:S(2)}) collective-permute-start(f32[1,4,3,128]{3,2,1,0:T(4,128)S(1)} %get-tuple-element.34), channel_id=1, source_target_pairs={{0,1},{1,2},{2,3},{3,4},{4,5},{5,6},{6,7},{7,0},{8,9},{9,10},{10,1... | collective-permute-start | bytes 18440 | tf_op jit(solution)/shard_map/ppermute | solution.py:15
  45.4 4.0 %collective-permute-start.11 = (f32[1,4,3,128]{3,2,1,0:T(4,128)S(1)}, f32[1,4,3,128]{3,2,1,0:T(4,128)S(1)}, u32[]{:S(2)}, u32[]{:S(2)}) collective-permute-start(f32[1,4,3,128]{3,2,1,0:T(4,128)S(1)} %get-tuple-element.35), channel_id=1, source_target_pairs={{1,0},{2,1},{3,2},{4,3},{5,4},{6,5},{7,6},{0,7},{9,8},{10,9},{11,1... | collective-permute-start | bytes 18440 | tf_op jit(solution)/shard_map/ppermute | solution.py:18
  60.1 2.6 %collective-permute-start.12 = (f32[1,1,128,16]{2,3,1,0:T(8,128)S(1)}, f32[1,1,128,16]{2,3,1,0:T(8,128)S(1)}, u32[]{:S(2)}, u32[]{:S(2)}) collective-permute-start(f32[1,1,128,16]{2,3,1,0:T(8,128)S(1)} %get-tuple-element.31), channel_id=1, source_target_pairs={{0,8},{8,16},{16,24},{1,9},{9,17},{17,25},{2,10},{10,18},{18,26},{... | collective-permute-start | bytes 24584 | tf_op jit(solution)/shard_map/ppermute | solution.py:26
  61.4 5.5 %collective-permute-start.13 = (f32[1,1,128,16]{2,3,1,0:T(8,128)S(1)}, f32[1,1,128,16]{2,3,1,0:T(8,128)S(1)}, u32[]{:S(2)}, u32[]{:S(2)}) collective-permute-start(f32[1,1,128,16]{2,3,1,0:T(8,128)S(1)} %get-tuple-element.32), channel_id=1, source_target_pairs={{8,0},{16,8},{24,16},{9,1},{17,9},{25,17},{10,2},{18,10},{26,18},{... | collective-permute-start | bytes 24584 | tf_op jit(solution)/shard_map/ppermute | solution.py:26
where the time goes:
time: 68 us; the launch traced here: 67.6 us
  starting transfers between devices  29.2 us (43%)
  waiting for transfers between devices  20.7 us (30%)
  blocking collectives  8.51 us (13%)
  local copies, waits for them, and re-layouts  4.84 us (7%)
  other arithmetic  3.95 us (6%)
    ppermute x8, starting transfers between devices, from_behind(): return lax.ppermute(shard, axis, pairs)  15.7 us
    ppermute x8, waiting for transfers between devices, from_behind(): return lax.ppermute(shard, axis, pairs)  13 us
    all_to_all x1, blocking collectives, relayout(): lax.all_to_all(block, 'lon', split_axis=3, concat_axis=2, tiled=True)  8.51 us
    ppermute x3, starting transfers between devices, extended_2(): lax.ppermute(lax.slice_in_dim(block, 0, width, axis=dim), axis, backward)  7.9 us
    all_to_all x1, waiting for transfers between devices, relayout(): lax.all_to_all(block, 'lon', split_axis=3, concat_axis=2, tiled=True)  4.84 us
    all_to_all x1, starting transfers between devices, relayout(): lax.all_to_all(block, 'lon', split_axis=3, concat_axis=2, tiled=True)  4.63 us
    ppermute x3, waiting for transfers between devices, extended_2(): lax.ppermute(lax.slice_in_dim(block, block.shape[dim] - width, None, axis...  2.77 us
    unnamed x15, local copies, waits for them, and re-layouts  2.15 us
  transfers between devices with their start and end apart: 15, of which 8 were waited for; matrix products, arithmetic and copies ran while one was open for 0% of the time, Pallas kernels for 0%

commit v1 on v0

--- a/solution.py
+++ b/solution.py
@@ -63,7 +63,10 @@
 def relayout(block, reach_rows):
     row_count = block.shape[0]
     lat_count = block.shape[1]
-    swapped = lax.all_to_all(block, "lon", split_axis=3, concat_axis=2, tiled=True)
+    swapped = jnp.concatenate(
+        lax.all_to_all(jnp.stack(jnp.split(block, lax.axis_size("lon"), axis=3)), "lon", 0, 0),
+        axis=2,
+    )
     lon_count = swapped.shape[2]
     col_count = swapped.shape[3]
     block_count = lat_count // row_count

time: 68 us -> 68.5 us (level)
    unnamed x15 -> x29, local copies, waits for them, and re-layouts: 2.15 us -> 2.77 us
where the time goes in v1:
time: 68.5 us; the launch traced here: 68 us
  starting transfers between devices  29.2 us (43%)
  waiting for transfers between devices  20.7 us (30%)
  blocking collectives  8.51 us (12%)
  local copies, waits for them, and re-layouts  5.29 us (8%)
  other arithmetic  3.94 us (6%)
    ppermute x8, starting transfers between devices, from_behind(): return lax.ppermute(shard, axis, pairs)  15.7 us
    ppermute x8, waiting for transfers between devices, from_behind(): return lax.ppermute(shard, axis, pairs)  13 us
    all_to_all x1, blocking collectives, relayout(): lax.all_to_all(jnp.stack(jnp.split(block, lax.axis_size('lon'), axis=3)),...  8.51 us
    ppermute x3, starting transfers between devices, extended_2(): lax.ppermute(lax.slice_in_dim(block, 0, width, axis=dim), axis, backward)  7.9 us
    all_to_all x1, waiting for transfers between devices, relayout(): lax.all_to_all(jnp.stack(jnp.split(block, lax.axis_size('lon'), axis=3)),...  4.84 us
    all_to_all x1, starting transfers between devices, relayout(): lax.all_to_all(jnp.stack(jnp.split(block, lax.axis_size('lon'), axis=3)),...  4.63 us
    ppermute x3, waiting for transfers between devices, extended_2(): lax.ppermute(lax.slice_in_dim(block, block.shape[dim] - width, None, axis...  2.77 us
    unnamed x29, local copies, waits for them, and re-layouts  2.77 us
  transfers between devices with their start and end apart: 15, of which 8 were waited for; matrix products, arithmetic and copies ran while one was open for 0% of the time, Pallas kernels for 0%

profile of v1, /device:TPU:0, one launch (start us, length us, event | category | flops | bytes accessed | tf_op | source)
XLA Modules:
  0.0 68.0 jit_solution(759158874249953331)
XLA Ops:
  0.0 0.7 copy-done.2
  0.7 0.6 dynamic_slice.34
  1.2 0.7 fusion.50
  1.9 0.8 %broadcast_select_fusion = f32[1,4,16,128]{3,2,1,0:T(8,128)S(1)} fusion(f32[1,4,16,128]{3,2,1,0:T(8,128)} %param.4, pred[4]{0:T(512)(128)(4,1)S(1)} %get-tuple-element.51), kind=kLoop, calls=%fused_computation.118 | loop fusion | flops 8192 | bytes 65540 | tf_op jit(solution)/shard_map/jit(_where)/select_n | solution.py:114
  2.7 0.5 collective-permute-start
  3.3 2.9 %collective-permute-start.1 = (f32[1,4,3,128]{3,2,1,0:T(4,128)S(1)}, f32[1,4,3,128]{3,2,1,0:T(4,128)S(1)}, u32[]{:S(2)}, u32[]{:S(2)}) collective-permute-start(f32[1,4,3,128]{3,2,1,0:T(4,128)S(1)} %get-tuple-element.44), channel_id=1, source_target_pairs={{1,0},{2,1},{3,2},{4,3},{5,4},{6,5},{7,6},{0,7},{9,8},{10,9},{11,1... | collective-permute-start | bytes 18440 | tf_op jit(solution)/shard_map/ppermute | solution.py:18
  6.3 0.3 collective-permute-start.2
  6.6 2.3 %collective-permute-start.3 = (f32[7,4,3]{2,1,0:T(4,128)S(1)}, f32[7,4,3]{2,1,0:T(4,128)S(1)}, u32[]{:S(2)}, u32[]{:S(2)}) collective-permute-start(f32[7,4,3]{2,1,0:T(4,128)S(1)} %get-tuple-element.46), channel_id=1, source_target_pairs={{1,0},{2,1},{3,2},{4,3},{5,4},{6,5},{7,6},{0,7},{9,8},{10,9},{11,1... | collective-permute-start | bytes 1016 | tf_op jit(solution)/shard_map/ppermute | solution.py:18
  9.0 1.4 %collective-permute-done.2 = f32[7,4,3]{2,1,0:T(4,128)S(1)} collective-permute-done((f32[7,4,3]{2,1,0:T(4,128)S(1)}, f32[7,4,3]{2,1,0:T(4,128)S(1)}, u32[]{:S(2)}, u32[]{:S(2)}) %collective-permute-start.2) | collective-permute-done | bytes 368 | tf_op jit(solution)/shard_map/ppermute | solution.py:15
  10.5 0.1 maximum_bitcast_fusion.4
  10.6 0.1 fusion.4
  10.8 0.1 fusion.12
  10.9 0.1 fusion.36
  11.3 0.1 constant_dynamic-update-slice_fusion.3
  11.4 0.1 constant_dynamic-update-slice_fusion.2
  11.6 0.8 %reshape.184 = f32[8,1,1024]{2,1,0:T(1,128)} reshape(f32[8,1,4,16,16]{4,3,2,1,0:T(8,128)S(1)} %constant_dynamic-update-slice_fusion) | data formatting | bytes 65536
  12.4 4.6 %all-to-all-start = ((f32[8,1,1024]{2,1,0:T(1,128)}), f32[8,1,1024]{2,1,0:T(1,128)S(1)}, u32[]{:S(2)}, u32[]{:S(2)}) async-start(f32[8,1,1024]{2,1,0:T(1,128)} %reshape.184), calls=%async_computation | async-start | bytes 65536 | tf_op jit(solution)/shard_map/all_to_all | solution.py:67
  17.0 4.8 %all-to-all-done = f32[8,1,1024]{2,1,0:T(1,128)S(1)} async-done(((f32[8,1,1024]{2,1,0:T(1,128)}), f32[8,1,1024]{2,1,0:T(1,128)S(1)}, u32[]{:S(2)}, u32[]{:S(2)}) %all-to-all-start) | async-done | bytes 32800 | tf_op jit(solution)/shard_map/all_to_all | solution.py:67
  21.8 0.5 broadcast.178
  22.4 0.7 %reduce = f32[8,1024]{1,0:T(8,128)S(1)} reduce(f32[8,1,1024]{2,1,0:T(1,128)S(1)} %all-to-all-done, f32[]{:T(128)} %broadcast.178), dimensions={1}, to_apply=%all_to_all.6.reduce_sub_computation | reduce | bytes 65540 | tf_op jit(solution)/shard_map/all_to_all | solution.py:67
  23.1 0.1 reshape.185
  23.2 0.1 copy.6
  23.4 0.1 reshape_reshape.6
  23.5 5.5 %collective-permute-start.4 = (f32[1,1,128,16]{2,3,1,0:T(8,128)S(1)}, f32[1,1,128,16]{2,3,1,0:T(8,128)S(1)}, u32[]{:S(2)}, u32[]{:S(2)}) collective-permute-start(f32[1,1,128,16]{2,3,1,0:T(8,128)S(1)} %get-tuple-element.42), channel_id=1, source_target_pairs={{0,24},{1,25},{2,26},{3,27},{4,28},{5,29},{6,30},{7,31}} | collective-permute-start | bytes 24584 | tf_op jit(solution)/shard_map/ppermute | solution.py:26
  29.0 1.3 %collective-permute-start.5 = (f32[1,1,128,16]{2,3,1,0:T(8,128)S(1)}, f32[1,1,128,16]{2,3,1,0:T(8,128)S(1)}, u32[]{:S(2)}, u32[]{:S(2)}) collective-permute-start(f32[1,1,128,16]{2,3,1,0:T(8,128)S(1)} %get-tuple-element.41), channel_id=1, source_target_pairs={{0,16},{8,24},{1,17},{9,25},{2,18},{10,26},{3,19},{11,27},{4,20},{... | collective-permute-start | bytes 24584 | tf_op jit(solution)/shard_map/ppermute | solution.py:26
  30.3 2.5 %collective-permute-start.6 = (f32[1,1,128,16]{2,3,1,0:T(8,128)S(1)}, f32[1,1,128,16]{2,3,1,0:T(8,128)S(1)}, u32[]{:S(2)}, u32[]{:S(2)}) collective-permute-start(f32[1,1,128,16]{2,3,1,0:T(8,128)S(1)} %get-tuple-element.40), channel_id=1, source_target_pairs={{0,8},{8,16},{16,24},{1,9},{9,17},{17,25},{2,10},{10,18},{18,26},{... | collective-permute-start | bytes 24584 | tf_op jit(solution)/shard_map/ppermute | solution.py:26
  32.9 1.3 %collective-permute-done.6 = f32[1,1,128,16]{2,3,1,0:T(8,128)S(1)} collective-permute-done((f32[1,1,128,16]{2,3,1,0:T(8,128)S(1)}, f32[1,1,128,16]{2,3,1,0:T(8,128)S(1)}, u32[]{:S(2)}, u32[]{:S(2)}) %collective-permute-start.6) | collective-permute-done | bytes 8224 | tf_op jit(solution)/shard_map/ppermute | solution.py:26
  34.2 1.3 %collective-permute-start.7 = (f32[1,1,128,16]{2,3,1,0:T(8,128)S(1)}, f32[1,1,128,16]{2,3,1,0:T(8,128)S(1)}, u32[]{:S(2)}, u32[]{:S(2)}) collective-permute-start(f32[1,1,128,16]{2,3,1,0:T(8,128)S(1)} %get-tuple-element.38), channel_id=1, source_target_pairs={{8,0},{16,8},{24,16},{9,1},{17,9},{25,17},{10,2},{18,10},{26,18},{... | collective-permute-start | bytes 24584 | tf_op jit(solution)/shard_map/ppermute | solution.py:26
  35.5 1.3 %collective-permute-start.8 = (f32[1,1,128,16]{2,3,1,0:T(8,128)S(1)}, f32[1,1,128,16]{2,3,1,0:T(8,128)S(1)}, u32[]{:S(2)}, u32[]{:S(2)}) collective-permute-start(f32[1,1,128,16]{2,3,1,0:T(8,128)S(1)} %get-tuple-element.37), channel_id=1, source_target_pairs={{16,0},{24,8},{17,1},{25,9},{18,2},{26,10},{19,3},{27,11},{20,4},{... | collective-permute-start | bytes 24584 | tf_op jit(solution)/shard_map/ppermute | solution.py:26
  36.8 1.3 %collective-permute-start.9 = (f32[1,1,128,16]{2,3,1,0:T(8,128)S(1)}, f32[1,1,128,16]{2,3,1,0:T(8,128)S(1)}, u32[]{:S(2)}, u32[]{:S(2)}) collective-permute-start(f32[1,1,128,16]{2,3,1,0:T(8,128)S(1)} %get-tuple-element.36), channel_id=1, source_target_pairs={{24,0},{25,1},{26,2},{27,3},{28,4},{29,5},{30,6},{31,7}} | collective-permute-start | bytes 24584 | tf_op jit(solution)/shard_map/ppermute | solution.py:26
  38.1 1.9 %collective-permute-done.7 = f32[1,1,128,16]{2,3,1,0:T(8,128)S(1)} collective-permute-done((f32[1,1,128,16]{2,3,1,0:T(8,128)S(1)}, f32[1,1,128,16]{2,3,1,0:T(8,128)S(1)}, u32[]{:S(2)}, u32[]{:S(2)}) %collective-permute-start.7) | collective-permute-done | bytes 8224 | tf_op jit(solution)/shard_map/ppermute | solution.py:26
  40.0 2.7 %collective-permute-done.8 = f32[1,1,128,16]{2,3,1,0:T(8,128)S(1)} collective-permute-done((f32[1,1,128,16]{2,3,1,0:T(8,128)S(1)}, f32[1,1,128,16]{2,3,1,0:T(8,128)S(1)}, u32[]{:S(2)}, u32[]{:S(2)}) %collective-permute-start.8) | collective-permute-done | bytes 8224 | tf_op jit(solution)/shard_map/ppermute | solution.py:26
  42.7 2.8 %collective-permute-done.9 = f32[1,1,128,16]{2,3,1,0:T(8,128)S(1)} collective-permute-done((f32[1,1,128,16]{2,3,1,0:T(8,128)S(1)}, f32[1,1,128,16]{2,3,1,0:T(8,128)S(1)}, u32[]{:S(2)}, u32[]{:S(2)}) %collective-permute-start.9) | collective-permute-done | bytes 8224 | tf_op jit(solution)/shard_map/ppermute | solution.py:26
  45.7 2.6 %collective-permute-start.11 = (f32[1,4,3,128]{3,2,1,0:T(4,128)S(1)}, f32[1,4,3,128]{3,2,1,0:T(4,128)S(1)}, u32[]{:S(2)}, u32[]{:S(2)}) collective-permute-start(f32[1,4,3,128]{3,2,1,0:T(4,128)S(1)} %get-tuple-element.35), channel_id=1, source_target_pairs={{1,0},{2,1},{3,2},{4,3},{5,4},{6,5},{7,6},{0,7},{9,8},{10,9},{11,1... | collective-permute-start | bytes 18440 | tf_op jit(solution)/shard_map/ppermute | solution.py:18
  48.3 1.4 %collective-permute-done.10 = f32[1,4,3,128]{3,2,1,0:T(4,128)S(1)} collective-permute-done((f32[1,4,3,128]{3,2,1,0:T(4,128)S(1)}, f32[1,4,3,128]{3,2,1,0:T(4,128)S(1)}, u32[]{:S(2)}, u32[]{:S(2)}) %collective-permute-start.10) | collective-permute-done | bytes 6176 | tf_op jit(solution)/shard_map/ppermute | solution.py:15
  49.7 0.1 fusion.20
  49.9 0.1 fusion.28
  50.0 0.1 fusion.45
  50.7 0.2 reshape.186
  50.9 8.5 %all_to_all.10 = f32[8,1,1024]{2,1,0:T(1,128)S(1)} all-to-all(f32[8,1,1024]{2,1,0:T(1,128)S(1)} %reshape.186), channel_id=1, replica_groups=mesh['lat'=4,'lon'=8] {'lon'}, dimensions={0} | all-to-all | bytes 65536 | tf_op jit(solution)/shard_map/all_to_all | solution.py:67
  59.4 0.7 %reduce.1 = f32[8,1024]{1,0:T(8,128)S(1)} reduce(f32[8,1,1024]{2,1,0:T(1,128)S(1)} %all_to_all.10, f32[]{:T(128)} %broadcast.178), dimensions={1}, to_apply=%all_to_all.7.reduce_sub_computation | reduce | bytes 65540 | tf_op jit(solution)/shard_map/all_to_all | solution.py:67
  60.1 0.1 reshape.187
  60.2 0.1 copy.8
  60.4 0.1 reshape_reshape.7
  60.5 1.3 %collective-permute-start.12 = (f32[1,1,128,16]{2,3,1,0:T(8,128)S(1)}, f32[1,1,128,16]{2,3,1,0:T(8,128)S(1)}, u32[]{:S(2)}, u32[]{:S(2)}) collective-permute-start(f32[1,1,128,16]{2,3,1,0:T(8,128)S(1)} %get-tuple-element.31), channel_id=1, source_target_pairs={{0,8},{8,16},{16,24},{1,9},{9,17},{17,25},{2,10},{10,18},{18,26},{... | collective-permute-start | bytes 24584 | tf_op jit(solution)/shard_map/ppermute | solution.py:26
  61.8 1.3 %collective-permute-start.13 = (f32[1,1,128,16]{2,3,1,0:T(8,128)S(1)}, f32[1,1,128,16]{2,3,1,0:T(8,128)S(1)}, u32[]{:S(2)}, u32[]{:S(2)}) collective-permute-start(f32[1,1,128,16]{2,3,1,0:T(8,128)S(1)} %get-tuple-element.32), channel_id=1, source_target_pairs={{8,0},{16,8},{24,16},{9,1},{17,9},{25,17},{10,2},{18,10},{26,18},{... | collective-permute-start | bytes 24584 | tf_op jit(solution)/shard_map/ppermute | solution.py:26
  63.2 4.2 %collective-permute-done.13 = f32[1,1,128,16]{2,3,1,0:T(8,128)S(1)} collective-permute-done((f32[1,1,128,16]{2,3,1,0:T(8,128)S(1)}, f32[1,1,128,16]{2,3,1,0:T(8,128)S(1)}, u32[]{:S(2)}, u32[]{:S(2)}) %collective-permute-start.13) | collective-permute-done | bytes 8224 | tf_op jit(solution)/shard_map/ppermute | solution.py:26
  67.4 0.6 slice_bitcast_fusion
  (56 shorter events, 1.4 us)
Async XLA Ops:
  0.0 0.7 copy-start.2
  2.7 3.5 %copy-start = (f32[2,3,4,16]{3,2,1,0:T(4,128)S(1)}, f32[2,3,4,16]{3,2,1,0:T(4,128)}, u32[]{:S(2)}) copy-start(f32[2,3,4,16]{3,2,1,0:T(4,128)} %param.5) | copy-start | bytes 4612
  2.7 7.8 %collective-permute-start = (f32[1,4,3,128]{3,2,1,0:T(4,128)S(1)}, f32[1,4,3,128]{3,2,1,0:T(4,128)S(1)}, u32[]{:S(2)}, u32[]{:S(2)}) collective-permute-start(f32[1,4,3,128]{3,2,1,0:T(4,128)S(1)} %get-tuple-element.43), channel_id=1, source_target_pairs={{0,1},{1,2},{2,3},{3,4},{4,5},{5,6},{6,7},{7,0},{8,9},{9,10},{10,1... | collective-permute-start | bytes 18440 | tf_op jit(solution)/shard_map/ppermute | solution.py:15
  3.3 3.0 %copy-start.1 = (f32[4,16]{1,0:T(4,128)S(1)}, f32[4,16]{1,0:T(4,128)}, u32[]{:S(2)}) copy-start(f32[4,16]{1,0:T(4,128)} %param.6) | copy-start | bytes 772
  3.3 7.3 %collective-permute-start.1 = (f32[1,4,3,128]{3,2,1,0:T(4,128)S(1)}, f32[1,4,3,128]{3,2,1,0:T(4,128)S(1)}, u32[]{:S(2)}, u32[]{:S(2)}) collective-permute-start(f32[1,4,3,128]{3,2,1,0:T(4,128)S(1)} %get-tuple-element.44), channel_id=1, source_target_pairs={{1,0},{2,1},{3,2},{4,3},{5,4},{6,5},{7,6},{0,7},{9,8},{10,9},{11,1... | collective-permute-start | bytes 18440 | tf_op jit(solution)/shard_map/ppermute | solution.py:18
  6.3 4.0 %collective-permute-start.2 = (f32[7,4,3]{2,1,0:T(4,128)S(1)}, f32[7,4,3]{2,1,0:T(4,128)S(1)}, u32[]{:S(2)}, u32[]{:S(2)}) collective-permute-start(f32[7,4,3]{2,1,0:T(4,128)S(1)} %get-tuple-element.45), channel_id=1, source_target_pairs={{0,1},{1,2},{2,3},{3,4},{4,5},{5,6},{6,7},{7,0},{8,9},{9,10},{10,1... | collective-permute-start | bytes 1016 | tf_op jit(solution)/shard_map/ppermute | solution.py:15
  6.6 3.8 %collective-permute-start.3 = (f32[7,4,3]{2,1,0:T(4,128)S(1)}, f32[7,4,3]{2,1,0:T(4,128)S(1)}, u32[]{:S(2)}, u32[]{:S(2)}) collective-permute-start(f32[7,4,3]{2,1,0:T(4,128)S(1)} %get-tuple-element.46), channel_id=1, source_target_pairs={{1,0},{2,1},{3,2},{4,3},{5,4},{6,5},{7,6},{0,7},{9,8},{10,9},{11,1... | collective-permute-start | bytes 1016 | tf_op jit(solution)/shard_map/ppermute | solution.py:18
  12.4 9.5 %all-to-all-start = ((f32[8,1,1024]{2,1,0:T(1,128)}), f32[8,1,1024]{2,1,0:T(1,128)S(1)}, u32[]{:S(2)}, u32[]{:S(2)}) async-start(f32[8,1,1024]{2,1,0:T(1,128)} %reshape.184), calls=%async_computation | async-start | bytes 65536 | tf_op jit(solution)/shard_map/all_to_all | solution.py:67
  23.5 9.3 %collective-permute-start.4 = (f32[1,1,128,16]{2,3,1,0:T(8,128)S(1)}, f32[1,1,128,16]{2,3,1,0:T(8,128)S(1)}, u32[]{:S(2)}, u32[]{:S(2)}) collective-permute-start(f32[1,1,128,16]{2,3,1,0:T(8,128)S(1)} %get-tuple-element.42), channel_id=1, source_target_pairs={{0,24},{1,25},{2,26},{3,27},{4,28},{5,29},{6,30},{7,31}} | collective-permute-start | bytes 24584 | tf_op jit(solution)/shard_map/ppermute | solution.py:26
  29.0 3.8 %collective-permute-start.5 = (f32[1,1,128,16]{2,3,1,0:T(8,128)S(1)}, f32[1,1,128,16]{2,3,1,0:T(8,128)S(1)}, u32[]{:S(2)}, u32[]{:S(2)}) collective-permute-start(f32[1,1,128,16]{2,3,1,0:T(8,128)S(1)} %get-tuple-element.41), channel_id=1, source_target_pairs={{0,16},{8,24},{1,17},{9,25},{2,18},{10,26},{3,19},{11,27},{4,20},{... | collective-permute-start | bytes 24584 | tf_op jit(solution)/shard_map/ppermute | solution.py:26
  30.3 3.8 %collective-permute-start.6 = (f32[1,1,128,16]{2,3,1,0:T(8,128)S(1)}, f32[1,1,128,16]{2,3,1,0:T(8,128)S(1)}, u32[]{:S(2)}, u32[]{:S(2)}) collective-permute-start(f32[1,1,128,16]{2,3,1,0:T(8,128)S(1)} %get-tuple-element.40), channel_id=1, source_target_pairs={{0,8},{8,16},{16,24},{1,9},{9,17},{17,25},{2,10},{10,18},{18,26},{... | collective-permute-start | bytes 24584 | tf_op jit(solution)/shard_map/ppermute | solution.py:26
  34.2 5.8 %collective-permute-start.7 = (f32[1,1,128,16]{2,3,1,0:T(8,128)S(1)}, f32[1,1,128,16]{2,3,1,0:T(8,128)S(1)}, u32[]{:S(2)}, u32[]{:S(2)}) collective-permute-start(f32[1,1,128,16]{2,3,1,0:T(8,128)S(1)} %get-tuple-element.38), channel_id=1, source_target_pairs={{8,0},{16,8},{24,16},{9,1},{17,9},{25,17},{10,2},{18,10},{26,18},{... | collective-permute-start | bytes 24584 | tf_op jit(solution)/shard_map/ppermute | solution.py:26
  35.5 7.3 %collective-permute-start.8 = (f32[1,1,128,16]{2,3,1,0:T(8,128)S(1)}, f32[1,1,128,16]{2,3,1,0:T(8,128)S(1)}, u32[]{:S(2)}, u32[]{:S(2)}) collective-permute-start(f32[1,1,128,16]{2,3,1,0:T(8,128)S(1)} %get-tuple-element.37), channel_id=1, source_target_pairs={{16,0},{24,8},{17,1},{25,9},{18,2},{26,10},{19,3},{27,11},{20,4},{... | collective-permute-start | bytes 24584 | tf_op jit(solution)/shard_map/ppermute | solution.py:26
  36.8 8.8 %collective-permute-start.9 = (f32[1,1,128,16]{2,3,1,0:T(8,128)S(1)}, f32[1,1,128,16]{2,3,1,0:T(8,128)S(1)}, u32[]{:S(2)}, u32[]{:S(2)}) collective-permute-start(f32[1,1,128,16]{2,3,1,0:T(8,128)S(1)} %get-tuple-element.36), channel_id=1, source_target_pairs={{24,0},{25,1},{26,2},{27,3},{28,4},{29,5},{30,6},{31,7}} | collective-permute-start | bytes 24584 | tf_op jit(solution)/shard_map/ppermute | solution.py:26
  45.6 4.1 %collective-permute-start.10 = (f32[1,4,3,128]{3,2,1,0:T(4,128)S(1)}, f32[1,4,3,128]{3,2,1,0:T(4,128)S(1)}, u32[]{:S(2)}, u32[]{:S(2)}) collective-permute-start(f32[1,4,3,128]{3,2,1,0:T(4,128)S(1)} %get-tuple-element.34), channel_id=1, source_target_pairs={{0,1},{1,2},{2,3},{3,4},{4,5},{5,6},{6,7},{7,0},{8,9},{9,10},{10,1... | collective-permute-start | bytes 18440 | tf_op jit(solution)/shard_map/ppermute | solution.py:15
  45.7 4.0 %collective-permute-start.11 = (f32[1,4,3,128]{3,2,1,0:T(4,128)S(1)}, f32[1,4,3,128]{3,2,1,0:T(4,128)S(1)}, u32[]{:S(2)}, u32[]{:S(2)}) collective-permute-start(f32[1,4,3,128]{3,2,1,0:T(4,128)S(1)} %get-tuple-element.35), channel_id=1, source_target_pairs={{1,0},{2,1},{3,2},{4,3},{5,4},{6,5},{7,6},{0,7},{9,8},{10,9},{11,1... | collective-permute-start | bytes 18440 | tf_op jit(solution)/shard_map/ppermute | solution.py:18
  60.5 2.6 %collective-permute-start.12 = (f32[1,1,128,16]{2,3,1,0:T(8,128)S(1)}, f32[1,1,128,16]{2,3,1,0:T(8,128)S(1)}, u32[]{:S(2)}, u32[]{:S(2)}) collective-permute-start(f32[1,1,128,16]{2,3,1,0:T(8,128)S(1)} %get-tuple-element.31), channel_id=1, source_target_pairs={{0,8},{8,16},{16,24},{1,9},{9,17},{17,25},{2,10},{10,18},{18,26},{... | collective-permute-start | bytes 24584 | tf_op jit(solution)/shard_map/ppermute | solution.py:26
  61.8 5.5 %collective-permute-start.13 = (f32[1,1,128,16]{2,3,1,0:T(8,128)S(1)}, f32[1,1,128,16]{2,3,1,0:T(8,128)S(1)}, u32[]{:S(2)}, u32[]{:S(2)}) collective-permute-start(f32[1,1,128,16]{2,3,1,0:T(8,128)S(1)} %get-tuple-element.32), channel_id=1, source_target_pairs={{8,0},{16,8},{24,16},{9,1},{17,9},{25,17},{10,2},{18,10},{26,18},{... | collective-permute-start | bytes 24584 | tf_op jit(solution)/shard_map/ppermute | solution.py:26
